TPU v7x, 32 devices: a whole 2x2x4 slice. The times are simulated.
32 devices in a mesh: section: 4 (over y, x), student: 2 (over core), dp: 4 (over z).
Axes of the slice: x: 2, y: 2, z: 4, core: 2. Of those that a mesh axis runs over, the one named last changes fastest.
Arguments:
- in_flight: bfloat16 [4, 2, 128, 4096], P('section', 'student'), may hold values from -6 to 6
- segments: int32 [4, 2, 128], P(None, 'student'), may hold values from 0 to 3, never falling along the last dimension, each value on 1 to 64 neighbouring positions
- norm_gain: float32 [4, 4096], P('section'), may hold values from 0.5 to 1.5
- w_qkv: bfloat16 [4, 4096, 3, 1024], P('section', None, None, 'dp')
- w_out: bfloat16 [4, 1024, 4096], P('section', 'dp'), may hold values from -0.1875 to 0.1875
- final_gain: float32 [4096], replicated, may hold values from 0.25 to 1.75
- student_rows: bfloat16 [2, 3, 2, 128, 1024], P('student', None, None, 'dp'), may hold values from -6 to 6
- student_gain: float32 [2, 1024], P('student'), may hold values from 0.5 to 1.5
- w_head: bfloat16 [2, 1024, 4096], P('student', None, 'section'), may hold values from -0.1875 to 0.1875
Outputs:
- advanced: bfloat16 [4, 2, 128, 4096], P('section', 'student', 'dp')
- grad_head: float32 [2, 1024, 4096], P('student', 'dp', 'section')
Inputs may be any that keep to these rules, and one draw needn't show every extreme that they name: `segments`: along a micro-batch's tokens the crop numbers never fall; each of the 4 crops holds 1 to 64 tokens and one holds exactly 64.
All inputs are finite; a program needn't handle non-finite values.
Results may differ from a plain program's by a relative error of at most 0.025.
Values may be sent and summed in bfloat16 or wider, within the bound.
A program may use at most 64 MiB of HBM per device.

v0:
```python
import jax
import jax.numpy as jnp
from jax import lax
from jax.sharding import PartitionSpec as P

HEAD_SIZE = 128
TOK = 128


def shifted(x, axis, by):
    count = lax.axis_size(axis)
    pairs = [(i, i + by) for i in range(count) if 0 <= i + by < count]
    return lax.ppermute(x, axis, pairs)


def broadcast(value, axis, source):
    kept = jnp.where(lax.axis_index(axis) == source, value, 0).astype(value.dtype)
    return lax.psum(kept, axis)


def layer_norm(rows, gain):
    rows = rows.astype(jnp.float32)
    centred = rows - jnp.mean(rows, axis=-1, keepdims=True)
    spread = jnp.mean(centred * centred, axis=-1, keepdims=True)
    return centred * lax.rsqrt(spread + 1e-06) * gain


def attend(state, crops, gain, weights_qkv, weights_out):
    tokens = state.shape[0]
    width = weights_out.shape[0]
    heads = width // HEAD_SIZE
    normed = layer_norm(state, gain).astype(jnp.bfloat16)
    qkv = jnp.dot(normed, weights_qkv, preferred_element_type=jnp.float32).astype(jnp.bfloat16)
    query = qkv[:, :width].reshape(tokens, heads, HEAD_SIZE)
    keys = qkv[:, width : 2 * width].reshape(tokens, heads, HEAD_SIZE)
    values = qkv[:, 2 * width :].reshape(tokens, heads, HEAD_SIZE)
    scores = jnp.einsum(
        "qhd,khd->hqk", query, keys, preferred_element_type=jnp.float32
    ) * HEAD_SIZE ** (-0.5)
    same = crops[:, None] == crops[None, :]
    scores = jnp.where(same[None], scores, -1e30)
    top = jnp.max(scores, axis=-1, keepdims=True)
    expo = jnp.exp(scores - top)
    probs = (expo / jnp.sum(expo, axis=-1, keepdims=True)).astype(jnp.bfloat16)
    mixed = jnp.einsum("hqk,khd->qhd", probs, values, preferred_element_type=jnp.float32).astype(
        jnp.bfloat16
    )
    return jnp.dot(mixed.reshape(tokens, width), weights_out, preferred_element_type=jnp.float32)


def on_device(
    in_flight, segments, norm_gain, w_qkv, w_out, final_gain, student_rows, student_gain, w_head
):
    section = lax.axis_index("section")
    root = lax.axis_size("section") - 1
    share = in_flight.shape[2] // lax.axis_size("dp")
    first_row = lax.axis_index("dp") * share
    ticks = student_rows.shape[1]
    model_width = in_flight.shape[3]
    weights_qkv = w_qkv[0].reshape(model_width, -1)
    weights_out = w_out[0]
    gain = norm_gain[0]
    crop_table = segments[:, 0, :]
    finals = []
    whole = in_flight[0, 0]
    own_rows = lax.dynamic_slice_in_dim(whole, first_row, share, 0)
    for tick in range(ticks):
        if tick > 0:
            whole = lax.all_gather(own_rows, "dp", axis=0, tiled=True)
        crops = lax.dynamic_index_in_dim(crop_table, section - tick, 0, keepdims=False)
        partial_value = attend(whole, crops, gain, weights_qkv, weights_out)
        summed = lax.psum_scatter(
            partial_value.astype(jnp.bfloat16), "dp", scatter_dimension=0, tiled=True
        ).astype(jnp.float32)
        own_rows = (own_rows.astype(jnp.float32) + summed).astype(jnp.bfloat16)
        finals.append(layer_norm(own_rows, final_gain).astype(jnp.bfloat16))
        own_rows = shifted(own_rows, "section", 1)
    advanced = own_rows[None, None]
    finished = jnp.stack(finals)[:, None]
    block = w_head.shape[2]
    block_start = section * block
    columns = lax.all_gather(finished, "student", axis=1, tiled=True)
    spread_rows = broadcast(columns, "section", root)
    targets = lax.dynamic_slice_in_dim(spread_rows, block_start, block, 3)
    student_width = student_rows.shape[4]
    feats = (
        layer_norm(student_rows[0], student_gain[0]).astype(jnp.bfloat16).reshape(-1, student_width)
    )
    pred = jnp.dot(feats, w_head[0], preferred_element_type=jnp.float32)
    err = ((pred - targets.reshape(-1, block).astype(jnp.float32)) * (2.0 / TOK)).astype(
        jnp.bfloat16
    )
    term = lax.dot_general(feats, err, (((0,), (0,)), ((), ())), preferred_element_type=jnp.float32)
    grad = lax.psum_scatter(
        term.astype(jnp.bfloat16), "dp", scatter_dimension=0, tiled=True
    ).astype(jnp.float32)
    return (advanced, grad[None])


def solution(mesh):
    in_specs = (
        P("section", "student", None, None),
        P(None, "student", None),
        P("section", None),
        P("section", None, None, "dp"),
        P("section", "dp", None),
        P(),
        P("student", None, None, "dp", None),
        P("student", None),
        P("student", None, "section"),
    )
    out_specs = (P("section", "student", "dp", None), P("student", "dp", "section"))
    return jax.shard_map(
        on_device, mesh=mesh, in_specs=in_specs, out_specs=out_specs, check_vma=False
    )
```

profile of v0, /device:TPU:0, one launch (start us, length us, event | category | flops | bytes accessed | tf_op | source)
XLA Modules:
  0.0 340.8 jit_solution(15224556704318031938)
XLA Ops:
  8.2 8.9 %copy.23 = bf16[1,4096,3,256]{1,3,2,0:T(8,128)(2,1)} copy(bf16[1,4096,3,256]{3,1,2,0:T(8,128)(2,1)} %param.12) | data formatting | bytes 12582912 | tf_op args[3]
  17.8 5.0 %convolution_convert_fusion.6 = bf16[128,768]{1,0:T(8,128)(2,1)S(1)} fusion(bf16[4096,768]{0,1:T(8,128)(2,1)} %bitcast.129, bf16[1,1,128,4096]{3,2,1,0:T(8,128)(2,1)S(1)} %copy-done.2, f32[4096]{0:T(1024)S(1)} %bitcast.144, f32[128]{0:T(128)S(1)} %add_rsqrt_fusion.6, f32[128]{0:T(128)S(1)} %broadcast_multiply_fusion.6), kind=kOutput, calls=%fused_computation.41 | convolution fusion | flops 808026112 | bytes 7554048 | tf_op jit(solution)/shard_map/dot_general | solution.py:33
  24.9 30.1 %reduce-scatter.5.cloned.1.call-done = bf16[32,4096]{1,0:T(8,128)(2,1)} async-done(((bf16[128,4096]{1,0:T(8,128)(2,1)}), bf16[32,4096]{1,0:T(8,128)(2,1)}) %reduce-scatter.5.cloned.1.call-update) | async-done | bytes 262160 | tf_op jit(solution)/shard_map/reduce_scatter | solution.py:72
  56.1 3.4 collective-permute-start
  59.5 5.1 %collective-permute-done = bf16[32,4096]{1,0:T(8,128)(2,1)S(1)} collective-permute-done((bf16[32,4096]{1,0:T(8,128)(2,1)S(1)}, bf16[32,4096]{1,0:T(8,128)(2,1)S(1)}, u32[]{:S(2)}, u32[]{:S(2)}) %collective-permute-start) | collective-permute-done | bytes 262176 | tf_op jit(solution)/shard_map/ppermute | solution.py:13
  65.6 27.8 %all-gather.5.cloned.1.call-done = bf16[128,4096]{1,0:T(8,128)(2,1)} async-done(((bf16[32,4096]{1,0:T(8,128)(2,1)}), bf16[128,4096]{1,0:T(8,128)(2,1)}) %all-gather.5.cloned.1.call-update) | async-done | bytes 1048592 | tf_op jit(solution)/shard_map/all_gather | solution.py:69
  93.4 1.5 convert_reduce_fusion.2
  95.0 1.7 fusion.10
  96.6 5.0 %convolution_convert_fusion.5 = bf16[128,768]{1,0:T(8,128)(2,1)S(1)} fusion(bf16[4096,768]{0,1:T(8,128)(2,1)} %bitcast.130, bf16[128,4096]{1,0:T(8,128)(2,1)S(1)} %copy-done.3, f32[4096]{0:T(1024)S(1)} %bitcast.145, f32[128]{0:T(128)S(1)} %add_rsqrt_fusion.5, f32[128]{0:T(128)S(1)} %broadcast_multiply_fusion.5), kind=kOutput, calls=%fused_computation.40 | convolution fusion | flops 808026112 | bytes 7554048 | tf_op jit(solution)/shard_map/dot_general | solution.py:33
  103.8 26.8 %reduce-scatter.7.cloned.1.call-done = bf16[32,4096]{1,0:T(8,128)(2,1)} async-done(((bf16[128,4096]{1,0:T(8,128)(2,1)}), bf16[32,4096]{1,0:T(8,128)(2,1)}) %reduce-scatter.7.cloned.1.call-update) | async-done | bytes 262160 | tf_op jit(solution)/shard_map/reduce_scatter | solution.py:72
  131.7 3.4 collective-permute-start.1
  135.1 5.1 %collective-permute-done.1 = bf16[32,4096]{1,0:T(8,128)(2,1)S(1)} collective-permute-done((bf16[32,4096]{1,0:T(8,128)(2,1)S(1)}, bf16[32,4096]{1,0:T(8,128)(2,1)S(1)}, u32[]{:S(2)}, u32[]{:S(2)}) %collective-permute-start.1) | collective-permute-done | bytes 262176 | tf_op jit(solution)/shard_map/ppermute | solution.py:13
  141.0 27.9 %all-gather.7.cloned.1.call-done = bf16[128,4096]{1,0:T(8,128)(2,1)} async-done(((bf16[32,4096]{1,0:T(8,128)(2,1)}), bf16[128,4096]{1,0:T(8,128)(2,1)}) %all-gather.7.cloned.1.call-update) | async-done | bytes 1048592 | tf_op jit(solution)/shard_map/all_gather | solution.py:69
  168.9 1.5 convert_reduce_fusion.1
  170.5 1.7 fusion.7
  172.1 5.0 %convolution_convert_fusion.4 = bf16[128,768]{1,0:T(8,128)(2,1)S(1)} fusion(bf16[4096,768]{0,1:T(8,128)(2,1)} %bitcast.131, bf16[128,4096]{1,0:T(8,128)(2,1)S(1)} %copy-done.4, f32[128]{0:T(128)S(1)} %add_rsqrt_fusion.4, f32[128]{0:T(128)S(1)} %broadcast_multiply_fusion.4, f32[4096]{0:T(1024)S(1)} %bitcast.146), kind=kOutput, calls=%fused_computation.39 | convolution fusion | flops 808026112 | bytes 7554048 | tf_op jit(solution)/shard_map/dot_general | solution.py:33
  179.8 26.2 %reduce-scatter.9.cloned.1.call-done = bf16[32,4096]{1,0:T(8,128)(2,1)} async-done(((bf16[128,4096]{1,0:T(8,128)(2,1)}), bf16[32,4096]{1,0:T(8,128)(2,1)}) %reduce-scatter.9.cloned.1.call-update) | async-done | bytes 262160 | tf_op jit(solution)/shard_map/reduce_scatter | solution.py:72
  208.8 8.4 %all-gather.9.cloned.1.call-done = bf16[3,64,4096]{2,1,0:T(8,128)(2,1)} async-done(((bf16[3,32,4096]{2,1,0:T(8,128)(2,1)}), bf16[3,64,4096]{2,1,0:T(8,128)(2,1)}) %all-gather.9.cloned.1.call-update) | async-done | bytes 1572880 | tf_op jit(solution)/shard_map/all_gather | solution.py:82
  219.7 62.6 %all-reduce.2.cloned.1.call-done = bf16[3,2,32,4096]{3,2,1,0:T(8,128)(2,1)} async-done(((bf16[3,2,32,4096]{3,2,1,0:T(8,128)(2,1)}), bf16[3,2,32,4096]{3,2,1,0:T(8,128)(2,1)}) %all-reduce.2.cloned.1.call-update) | async-done | bytes 1572880 | tf_op jit(solution)/shard_map/psum | solution.py:18
  283.3 4.1 %convolution_convert_fusion.3 = bf16[1024,1024]{1,0:T(8,128)(2,1)} fusion(bf16[192,1024]{1,0:T(8,128)(2,1)S(1)} %fusion.62, bf16[192,1024]{1,0:T(8,128)(2,1)S(1)} %bitcast.133, bf16[1,1024,1024]{2,1,0:T(8,128)(2,1)} %param.17, bf16[192,1024]{1,0:T(8,128)(2,1)S(1)} %bitcast.134), kind=kOutput, calls=%fused_computation.34 | convolution fusion | flops 807141376 | bytes 5373952 | tf_op jit(solution)/shard_map/dot_general | solution.py:93
  287.4 3.4 collective-permute-start.2
  290.8 5.4 %collective-permute-done.2 = bf16[32,4096]{1,0:T(8,128)(2,1)S(1)} collective-permute-done((bf16[32,4096]{1,0:T(8,128)(2,1)S(1)}, bf16[32,4096]{1,0:T(8,128)(2,1)S(1)}, u32[]{:S(2)}, u32[]{:S(2)}) %collective-permute-start.2) | collective-permute-done | bytes 262176 | tf_op jit(solution)/shard_map/ppermute | solution.py:13
  296.1 35.0 %reduce-scatter.11.cloned.1.call-done = bf16[256,1024]{1,0:T(8,128)(2,1)} async-done(((bf16[1024,1024]{1,0:T(8,128)(2,1)}), bf16[256,1024]{1,0:T(8,128)(2,1)}) %reduce-scatter.11.cloned.1.call-update) | async-done | bytes 524304 | tf_op jit(solution)/shard_map/reduce_scatter | solution.py:94
  331.2 2.1 bitcast_convert_fusion
  (94 shorter events, 19.2 us)
Async XLA Ops:
  7.2 16.2 %copy-start = (bf16[1,256,4096]{2,1,0:T(8,128)(2,1)S(1)}, bf16[1,256,4096]{2,1,0:T(8,128)(2,1)}, u32[]{:S(2)}) copy-start(bf16[1,256,4096]{2,1,0:T(8,128)(2,1)} %param.13) | copy-start | bytes 6291460
  7.2 47.8 %reduce-scatter.5.cloned.1.call-start = ((), (), s32[]{:S(2)}) async-start(), calls=%async_computation.4 | async-start | bytes 1310720 | tf_op jit(solution)/shard_map/reduce_scatter | solution.py:72
  8.2 8.9 %copy-start.2 = (bf16[1,1,128,4096]{3,2,1,0:T(8,128)(2,1)S(1)}, bf16[1,1,128,4096]{3,2,1,0:T(8,128)(2,1)}, u32[]{:S(2)}) copy-start(bf16[1,1,128,4096]{3,2,1,0:T(8,128)(2,1)} %param.9) | copy-start | bytes 3145732
  17.1 0.7 copy-start.11
  24.9 68.6 %all-gather.5.cloned.1.call-start = ((), (), s32[]{:S(2)}) async-start(), calls=%async_computation.5 | async-start | bytes 1310720 | tf_op jit(solution)/shard_map/all_gather | solution.py:69
  56.1 8.5 %collective-permute-start = (bf16[32,4096]{1,0:T(8,128)(2,1)S(1)}, bf16[32,4096]{1,0:T(8,128)(2,1)S(1)}, u32[]{:S(2)}, u32[]{:S(2)}) collective-permute-start(bf16[32,4096]{1,0:T(8,128)(2,1)S(1)} %get-tuple-element.3), channel_id=1, source_target_pairs={{0,8},{8,16},{16,24},{1,9},{9,17},{17,25},{2,10},{10,18},{18,26},{... | collective-permute-start | bytes 786440 | tf_op jit(solution)/shard_map/ppermute | solution.py:13
  64.7 0.7 copy-start.7
  65.4 65.1 %reduce-scatter.7.cloned.1.call-start = ((), (), s32[]{:S(2)}) async-start(), calls=%async_computation.6 | async-start | bytes 1310720 | tf_op jit(solution)/shard_map/reduce_scatter | solution.py:72
  93.4 3.2 copy-start.3
  102.2 28.3 %copy-start.8 = (bf16[32,4096]{1,0:T(8,128)(2,1)S(1)}, bf16[32,4096]{1,0:T(8,128)(2,1)}, u32[]{:S(2)}) copy-start(bf16[32,4096]{1,0:T(8,128)(2,1)} %copy-done.7) | copy-start | bytes 786436
  103.7 65.2 %all-gather.7.cloned.1.call-start = ((), (), s32[]{:S(2)}) async-start(), calls=%async_computation.7 | async-start | bytes 1310720 | tf_op jit(solution)/shard_map/all_gather | solution.py:69
  131.7 8.5 %collective-permute-start.1 = (bf16[32,4096]{1,0:T(8,128)(2,1)S(1)}, bf16[32,4096]{1,0:T(8,128)(2,1)S(1)}, u32[]{:S(2)}, u32[]{:S(2)}) collective-permute-start(bf16[32,4096]{1,0:T(8,128)(2,1)S(1)} %get-tuple-element.5), channel_id=1, source_target_pairs={{0,8},{8,16},{16,24},{1,9},{9,17},{17,25},{2,10},{10,18},{18,26},{... | collective-permute-start | bytes 786440 | tf_op jit(solution)/shard_map/ppermute | solution.py:13
  140.2 0.7 copy-start.5
  140.9 65.1 %reduce-scatter.9.cloned.1.call-start = ((), (), s32[]{:S(2)}) async-start(), calls=%async_computation.8 | async-start | bytes 1310720 | tf_op jit(solution)/shard_map/reduce_scatter | solution.py:72
  168.9 3.2 copy-start.4
  177.7 28.3 %copy-start.6 = (bf16[32,4096]{1,0:T(8,128)(2,1)S(1)}, bf16[32,4096]{1,0:T(8,128)(2,1)}, u32[]{:S(2)}) copy-start(bf16[32,4096]{1,0:T(8,128)(2,1)} %copy-done.5) | copy-start | bytes 786436
  179.2 28.3 %copy-start.9 = (f32[4096]{0:T(1024)S(1)}, f32[4096]{0:T(1024)}, u32[]{:S(2)}) copy-start(f32[4096]{0:T(1024)} %param.14) | copy-start | bytes 49156
  179.2 38.0 %all-gather.9.cloned.1.call-start = ((), (), s32[]{:S(2)}) async-start(), calls=%async_computation.11 | async-start | bytes 2359296 | tf_op jit(solution)/shard_map/all_gather | solution.py:82
  208.8 73.5 %all-reduce.2.cloned.1.call-start = ((), (), s32[]{:S(2)}) async-start(), calls=%async_computation.9 | async-start | bytes 3145728 | tf_op jit(solution)/shard_map/psum | solution.py:18
  208.8 9.7 %copy-start.1 = (bf16[1,3,2,32,1024]{4,3,2,1,0:T(8,128)(2,1)S(1)}, bf16[1,3,2,32,1024]{4,3,2,1,0:T(8,128)(2,1)}, u32[]{:S(2)}) copy-start(bf16[1,3,2,32,1024]{4,3,2,1,0:T(8,128)(2,1)} %param.15) | copy-start | bytes 1179652
  208.8 10.3 %copy-start.10 = (f32[1,1024]{1,0:T(1,128)S(1)}, f32[1,1024]{1,0:T(1,128)}, u32[]{:S(2)}) copy-start(f32[1,1024]{1,0:T(1,128)} %param.16) | copy-start | bytes 12292
  218.5 112.7 %reduce-scatter.11.cloned.1.call-start = ((), (), s32[]{:S(2)}) async-start(), calls=%async_computation.10 | async-start | bytes 2621440 | tf_op jit(solution)/shard_map/reduce_scatter | solution.py:94
  287.4 8.8 %collective-permute-start.2 = (bf16[32,4096]{1,0:T(8,128)(2,1)S(1)}, bf16[32,4096]{1,0:T(8,128)(2,1)S(1)}, u32[]{:S(2)}, u32[]{:S(2)}) collective-permute-start(bf16[32,4096]{1,0:T(8,128)(2,1)S(1)} %get-tuple-element.7), channel_id=1, source_target_pairs={{0,8},{8,16},{16,24},{1,9},{9,17},{17,25},{2,10},{10,18},{18,26},{... | collective-permute-start | bytes 786440 | tf_op jit(solution)/shard_map/ppermute | solution.py:13
Sparse Core Ops, SparseCore 0:
  25.0 29.9 reduce-scatter.4
  65.5 27.8 all-gather.4
  103.8 26.6 reduce-scatter.6
  141.1 27.8 all-gather.6
  179.3 26.6 reduce-scatter.8
  208.9 8.2 all-gather.8
  220.3 61.9 all-reduce.1
  287.5 43.6 reduce-scatter.10
where the time goes:
time: 342 us; the launch traced here: 341 us
  waiting for transfers between devices  261 us (76%)
  matrix products  24.5 us (7%)
  other arithmetic  17.2 us (5%)
  between operations  14.5 us (4%)
  local copies, waits for them, and re-layouts  13.5 us (4%)
  starting transfers between devices  10.5 us (3%)
    reduce_scatter x3, waiting for transfers between devices, on_device(): lax.psum_scatter(partial_value.astype(jnp.bfloat16), 'dp', scatter_dimens...  83.1 us
    psum x1, waiting for transfers between devices, broadcast(): return lax.psum(kept, axis)  62.6 us
    all_gather x2, waiting for transfers between devices, on_device(): whole = lax.all_gather(own_rows, 'dp', axis=0, tiled=True)  55.8 us
    reduce_scatter x1, waiting for transfers between devices, on_device(): lax.psum_scatter(term.astype(jnp.bfloat16), 'dp', scatter_dimension=0, ti...  35 us
    ppermute x3, waiting for transfers between devices, shifted(): return lax.ppermute(x, axis, pairs)  15.6 us
    dot_general x3, matrix products, attend(): jnp.dot(normed, weights_qkv, preferred_element_type=jnp.float32)  15.1 us
    unnamed x29, local copies, waits for them, and re-layouts  11.1 us
    ppermute x3, starting transfers between devices, shifted(): return lax.ppermute(x, axis, pairs)  10.2 us
  transfers between devices with their start and end apart: 11, of which 11 were waited for; matrix products, arithmetic and copies ran while one was open for 0% of the time, Pallas kernels for 0%

commit v1 on v0

--- a/solution.py
+++ b/solution.py
@@ -2,9 +2,11 @@
 import jax.numpy as jnp
 from jax import lax
 from jax.sharding import PartitionSpec as P
+from jax.lax import all_gather
 
 HEAD_SIZE = 128
 TOK = 128
+recast_thing = lambda arr, peer_axis: jnp.sum(all_gather(arr, axis_name=peer_axis), axis=0)
 
 
 def shifted(x, axis, by):
@@ -15,7 +17,7 @@
 
 def broadcast(value, axis, source):
     kept = jnp.where(lax.axis_index(axis) == source, value, 0).astype(value.dtype)
-    return lax.psum(kept, axis)
+    return recast_thing(kept, axis)
 
 
 def layer_norm(rows, gain):

time: 342 us -> 356 us (1.041)
  waiting for transfers between devices: 261 us -> 269 us
  other arithmetic: 17.2 us -> 22.8 us
    all_gather x0 -> x1, waiting for transfers between devices: none -> 71.4 us  [all_gather(arr, axis_name=peer_axis)]
    psum x1 -> x0, waiting for transfers between devices: 62.6 us -> none  [broadcast(): return lax.psum(kept, axis)]
    reduce_sum x0 -> x1, other arithmetic: none -> 5.58 us  [jnp.sum(all_gather(arr, axis_name=peer_axis), axis=0)]
where the time goes in v1:
time: 356 us; the launch traced here: 355 us
  waiting for transfers between devices  269 us (76%)
  matrix products  24.5 us (7%)
  other arithmetic  22.8 us (6%)
  between operations  14.5 us (4%)
  local copies, waits for them, and re-layouts  13.5 us (4%)
  starting transfers between devices  10.7 us (3%)
    reduce_scatter x3, waiting for transfers between devices, on_device(): lax.psum_scatter(partial_value.astype(jnp.bfloat16), 'dp', scatter_dimens...  83.1 us
    all_gather x1, waiting for transfers between devices, all_gather(arr, axis_name=peer_axis)  71.4 us
    all_gather x2, waiting for transfers between devices, on_device(): whole = lax.all_gather(own_rows, 'dp', axis=0, tiled=True)  55.8 us
    reduce_scatter x1, waiting for transfers between devices, on_device(): lax.psum_scatter(term.astype(jnp.bfloat16), 'dp', scatter_dimension=0, ti...  35 us
    ppermute x3, waiting for transfers between devices, shifted(): return lax.ppermute(x, axis, pairs)  15.6 us
    dot_general x3, matrix products, attend(): jnp.dot(normed, weights_qkv, preferred_element_type=jnp.float32)  15.1 us
    unnamed x29, local copies, waits for them, and re-layouts  11.1 us
    ppermute x3, starting transfers between devices, shifted(): return lax.ppermute(x, axis, pairs)  10.2 us
  transfers between devices with their start and end apart: 11, of which 11 were waited for; matrix products, arithmetic and copies ran while one was open for 0% of the time, Pallas kernels for 0%

profile of v1, /device:TPU:0, one launch (start us, length us, event | category | flops | bytes accessed | tf_op | source)
XLA Modules:
  0.0 355.4 jit_solution(2201067134488568034)
XLA Ops:
  8.2 8.9 %copy.36 = bf16[1,4096,3,256]{1,3,2,0:T(8,128)(2,1)} copy(bf16[1,4096,3,256]{3,1,2,0:T(8,128)(2,1)} %param.12) | data formatting | bytes 12582912 | tf_op args[3]
  17.8 5.0 %convolution_convert_fusion.6 = bf16[128,768]{1,0:T(8,128)(2,1)S(1)} fusion(bf16[4096,768]{0,1:T(8,128)(2,1)} %bitcast.130, bf16[1,1,128,4096]{3,2,1,0:T(8,128)(2,1)S(1)} %copy-done.2, f32[4096]{0:T(1024)S(1)} %bitcast.146, f32[128]{0:T(128)S(1)} %add_rsqrt_fusion.6, f32[128]{0:T(128)S(1)} %broadcast_multiply_fusion.6), kind=kOutput, calls=%fused_computation.41 | convolution fusion | flops 808026112 | bytes 7554048 | tf_op jit(solution)/shard_map/dot_general | solution.py:35
  24.9 30.1 %reduce-scatter.5.cloned.1.call-done = bf16[32,4096]{1,0:T(8,128)(2,1)} async-done(((bf16[128,4096]{1,0:T(8,128)(2,1)}), bf16[32,4096]{1,0:T(8,128)(2,1)}) %reduce-scatter.5.cloned.1.call-update) | async-done | bytes 262160 | tf_op jit(solution)/shard_map/reduce_scatter | solution.py:74
  56.1 3.4 collective-permute-start
  59.5 5.1 %collective-permute-done = bf16[32,4096]{1,0:T(8,128)(2,1)S(1)} collective-permute-done((bf16[32,4096]{1,0:T(8,128)(2,1)S(1)}, bf16[32,4096]{1,0:T(8,128)(2,1)S(1)}, u32[]{:S(2)}, u32[]{:S(2)}) %collective-permute-start) | collective-permute-done | bytes 262176 | tf_op jit(solution)/shard_map/ppermute | solution.py:15
  65.6 27.8 %all-gather.7.cloned.1.call-done = bf16[128,4096]{1,0:T(8,128)(2,1)} async-done(((bf16[32,4096]{1,0:T(8,128)(2,1)}), bf16[128,4096]{1,0:T(8,128)(2,1)}) %all-gather.7.cloned.1.call-update) | async-done | bytes 1048592 | tf_op jit(solution)/shard_map/all_gather | solution.py:71
  95.0 1.7 fusion.10
  96.6 5.0 %convolution_convert_fusion.5 = bf16[128,768]{1,0:T(8,128)(2,1)S(1)} fusion(bf16[4096,768]{0,1:T(8,128)(2,1)} %bitcast.131, bf16[128,4096]{1,0:T(8,128)(2,1)S(1)} %copy-done.3, f32[4096]{0:T(1024)S(1)} %bitcast.147, f32[128]{0:T(128)S(1)} %add_rsqrt_fusion.5, f32[128]{0:T(128)S(1)} %broadcast_multiply_fusion.5), kind=kOutput, calls=%fused_computation.40 | convolution fusion | flops 808026112 | bytes 7554048 | tf_op jit(solution)/shard_map/dot_general | solution.py:35
  103.8 26.7 %reduce-scatter.7.cloned.1.call-done = bf16[32,4096]{1,0:T(8,128)(2,1)} async-done(((bf16[128,4096]{1,0:T(8,128)(2,1)}), bf16[32,4096]{1,0:T(8,128)(2,1)}) %reduce-scatter.7.cloned.1.call-update) | async-done | bytes 262160 | tf_op jit(solution)/shard_map/reduce_scatter | solution.py:74
  131.6 3.4 collective-permute-start.1
  135.1 5.1 %collective-permute-done.1 = bf16[32,4096]{1,0:T(8,128)(2,1)S(1)} collective-permute-done((bf16[32,4096]{1,0:T(8,128)(2,1)S(1)}, bf16[32,4096]{1,0:T(8,128)(2,1)S(1)}, u32[]{:S(2)}, u32[]{:S(2)}) %collective-permute-start.1) | collective-permute-done | bytes 262176 | tf_op jit(solution)/shard_map/ppermute | solution.py:15
  141.0 27.9 %all-gather.9.cloned.1.call-done = bf16[128,4096]{1,0:T(8,128)(2,1)} async-done(((bf16[32,4096]{1,0:T(8,128)(2,1)}), bf16[128,4096]{1,0:T(8,128)(2,1)}) %all-gather.9.cloned.1.call-update) | async-done | bytes 1048592 | tf_op jit(solution)/shard_map/all_gather | solution.py:71
  168.9 1.5 convert_reduce_fusion.1
  170.5 1.7 fusion.7
  172.1 5.0 %convolution_convert_fusion.4 = bf16[128,768]{1,0:T(8,128)(2,1)S(1)} fusion(bf16[4096,768]{0,1:T(8,128)(2,1)} %bitcast.132, bf16[128,4096]{1,0:T(8,128)(2,1)S(1)} %copy-done.4, f32[128]{0:T(128)S(1)} %add_rsqrt_fusion.4, f32[128]{0:T(128)S(1)} %broadcast_multiply_fusion.4, f32[4096]{0:T(1024)S(1)} %bitcast.148), kind=kOutput, calls=%fused_computation.39 | convolution fusion | flops 808026112 | bytes 7554048 | tf_op jit(solution)/shard_map/dot_general | solution.py:35
  179.8 26.2 %reduce-scatter.9.cloned.1.call-done = bf16[32,4096]{1,0:T(8,128)(2,1)} async-done(((bf16[128,4096]{1,0:T(8,128)(2,1)}), bf16[32,4096]{1,0:T(8,128)(2,1)}) %reduce-scatter.9.cloned.1.call-update) | async-done | bytes 262160 | tf_op jit(solution)/shard_map/reduce_scatter | solution.py:74
  208.8 8.4 %all-gather.11.cloned.1.call-done = bf16[3,64,4096]{2,1,0:T(8,128)(2,1)} async-done(((bf16[3,32,4096]{2,1,0:T(8,128)(2,1)}), bf16[3,64,4096]{2,1,0:T(8,128)(2,1)}) %all-gather.11.cloned.1.call-update) | async-done | bytes 1572880 | tf_op jit(solution)/shard_map/all_gather | solution.py:84
  219.8 71.4 %all-gather.13.cloned.1.call-done = bf16[12,2,32,4096]{3,2,1,0:T(8,128)(2,1)} async-done(((bf16[3,2,32,4096]{3,2,1,0:T(8,128)(2,1)}), bf16[12,2,32,4096]{3,2,1,0:T(8,128)(2,1)}) %all-gather.13.cloned.1.call-update) | async-done | bytes 6291472 | tf_op jit(solution)/shard_map/all_gather | solution.py:9
  291.2 5.6 %reduce_sum.182 = bf16[3,2,32,4096]{3,2,1,0:T(8,128)(2,1)} reduce(bf16[4,3,2,32,4096]{4,3,2,1,0:T(8,128)(2,1)} %bitcast.133, bf16[]{:T(256)} %constant.73.clone.1), dimensions={0}, to_apply=%region_23.24 | reduce | flops 2359296 | bytes 7864322 | tf_op jit(solution)/shard_map/reduce_sum | solution.py:9
  297.8 4.1 %convolution_convert_fusion.3 = bf16[1024,1024]{1,0:T(8,128)(2,1)} fusion(bf16[192,1024]{1,0:T(8,128)(2,1)S(1)} %fusion.62, bf16[192,1024]{1,0:T(8,128)(2,1)S(1)} %bitcast.135, bf16[1,1024,1024]{2,1,0:T(8,128)(2,1)} %param.17, bf16[192,1024]{1,0:T(8,128)(2,1)S(1)} %bitcast.136), kind=kOutput, calls=%fused_computation.34 | convolution fusion | flops 807141376 | bytes 5373952 | tf_op jit(solution)/shard_map/dot_general | solution.py:95
  302.0 3.4 collective-permute-start.2
  305.4 5.4 %collective-permute-done.2 = bf16[32,4096]{1,0:T(8,128)(2,1)S(1)} collective-permute-done((bf16[32,4096]{1,0:T(8,128)(2,1)S(1)}, bf16[32,4096]{1,0:T(8,128)(2,1)S(1)}, u32[]{:S(2)}, u32[]{:S(2)}) %collective-permute-start.2) | collective-permute-done | bytes 262176 | tf_op jit(solution)/shard_map/ppermute | solution.py:15
  310.7 35.0 %reduce-scatter.11.cloned.1.call-done = bf16[256,1024]{1,0:T(8,128)(2,1)} async-done(((bf16[1024,1024]{1,0:T(8,128)(2,1)}), bf16[256,1024]{1,0:T(8,128)(2,1)}) %reduce-scatter.11.cloned.1.call-update) | async-done | bytes 524304 | tf_op jit(solution)/shard_map/reduce_scatter | solution.py:96
  345.7 2.1 bitcast_convert_fusion
  (95 shorter events, 20.9 us)
Async XLA Ops:
  7.2 16.2 %copy-start = (bf16[1,256,4096]{2,1,0:T(8,128)(2,1)S(1)}, bf16[1,256,4096]{2,1,0:T(8,128)(2,1)}, u32[]{:S(2)}) copy-start(bf16[1,256,4096]{2,1,0:T(8,128)(2,1)} %param.13) | copy-start | bytes 6291460
  7.2 47.8 %reduce-scatter.5.cloned.1.call-start = ((), (), s32[]{:S(2)}) async-start(), calls=%async_computation.4 | async-start | bytes 1310720 | tf_op jit(solution)/shard_map/reduce_scatter | solution.py:74
  8.2 8.9 %copy-start.2 = (bf16[1,1,128,4096]{3,2,1,0:T(8,128)(2,1)S(1)}, bf16[1,1,128,4096]{3,2,1,0:T(8,128)(2,1)}, u32[]{:S(2)}) copy-start(bf16[1,1,128,4096]{3,2,1,0:T(8,128)(2,1)} %param.9) | copy-start | bytes 3145732
  17.1 0.7 copy-start.11
  24.8 68.6 %all-gather.7.cloned.1.call-start = ((), (), s32[]{:S(2)}) async-start(), calls=%async_computation.5 | async-start | bytes 1310720 | tf_op jit(solution)/shard_map/all_gather | solution.py:71
  56.1 8.5 %collective-permute-start = (bf16[32,4096]{1,0:T(8,128)(2,1)S(1)}, bf16[32,4096]{1,0:T(8,128)(2,1)S(1)}, u32[]{:S(2)}, u32[]{:S(2)}) collective-permute-start(bf16[32,4096]{1,0:T(8,128)(2,1)S(1)} %get-tuple-element.3), channel_id=1, source_target_pairs={{0,8},{8,16},{16,24},{1,9},{9,17},{17,25},{2,10},{10,18},{18,26},{... | collective-permute-start | bytes 786440 | tf_op jit(solution)/shard_map/ppermute | solution.py:15
  64.7 0.7 copy-start.7
  65.4 65.1 %reduce-scatter.7.cloned.1.call-start = ((), (), s32[]{:S(2)}) async-start(), calls=%async_computation.6 | async-start | bytes 1310720 | tf_op jit(solution)/shard_map/reduce_scatter | solution.py:74
  93.4 3.2 copy-start.3
  102.2 28.3 %copy-start.8 = (bf16[32,4096]{1,0:T(8,128)(2,1)S(1)}, bf16[32,4096]{1,0:T(8,128)(2,1)}, u32[]{:S(2)}) copy-start(bf16[32,4096]{1,0:T(8,128)(2,1)} %copy-done.7) | copy-start | bytes 786436
  103.7 65.2 %all-gather.9.cloned.1.call-start = ((), (), s32[]{:S(2)}) async-start(), calls=%async_computation.7 | async-start | bytes 1310720 | tf_op jit(solution)/shard_map/all_gather | solution.py:71
  131.6 8.6 %collective-permute-start.1 = (bf16[32,4096]{1,0:T(8,128)(2,1)S(1)}, bf16[32,4096]{1,0:T(8,128)(2,1)S(1)}, u32[]{:S(2)}, u32[]{:S(2)}) collective-permute-start(bf16[32,4096]{1,0:T(8,128)(2,1)S(1)} %get-tuple-element.5), channel_id=1, source_target_pairs={{0,8},{8,16},{16,24},{1,9},{9,17},{17,25},{2,10},{10,18},{18,26},{... | collective-permute-start | bytes 786440 | tf_op jit(solution)/shard_map/ppermute | solution.py:15
  140.2 0.7 copy-start.5
  140.9 65.1 %reduce-scatter.9.cloned.1.call-start = ((), (), s32[]{:S(2)}) async-start(), calls=%async_computation.8 | async-start | bytes 1310720 | tf_op jit(solution)/shard_map/reduce_scatter | solution.py:74
  168.9 3.2 copy-start.4
  177.7 28.3 %copy-start.6 = (bf16[32,4096]{1,0:T(8,128)(2,1)S(1)}, bf16[32,4096]{1,0:T(8,128)(2,1)}, u32[]{:S(2)}) copy-start(bf16[32,4096]{1,0:T(8,128)(2,1)} %copy-done.5) | copy-start | bytes 786436
  179.2 28.3 %copy-start.9 = (f32[4096]{0:T(1024)S(1)}, f32[4096]{0:T(1024)}, u32[]{:S(2)}) copy-start(f32[4096]{0:T(1024)} %param.14) | copy-start | bytes 49156
  179.2 38.0 %all-gather.11.cloned.1.call-start = ((), (), s32[]{:S(2)}) async-start(), calls=%async_computation.10 | async-start | bytes 2359296 | tf_op jit(solution)/shard_map/all_gather | solution.py:84
  208.8 82.5 %all-gather.13.cloned.1.call-start = ((), (), s32[]{:S(2)}) async-start(), calls=%async_computation.11 | async-start | bytes 7864320 | tf_op jit(solution)/shard_map/all_gather | solution.py:9
  208.8 9.9 %copy-start.1 = (bf16[1,3,2,32,1024]{4,3,2,1,0:T(8,128)(2,1)S(1)}, bf16[1,3,2,32,1024]{4,3,2,1,0:T(8,128)(2,1)}, u32[]{:S(2)}) copy-start(bf16[1,3,2,32,1024]{4,3,2,1,0:T(8,128)(2,1)} %param.15) | copy-start | bytes 1179652
  208.8 10.5 %copy-start.10 = (f32[1,1024]{1,0:T(1,128)S(1)}, f32[1,1024]{1,0:T(1,128)}, u32[]{:S(2)}) copy-start(f32[1,1024]{1,0:T(1,128)} %param.16) | copy-start | bytes 12292
  218.5 127.3 %reduce-scatter.11.cloned.1.call-start = ((), (), s32[]{:S(2)}) async-start(), calls=%async_computation.9 | async-start | bytes 2621440 | tf_op jit(solution)/shard_map/reduce_scatter | solution.py:96
  302.0 8.8 %collective-permute-start.2 = (bf16[32,4096]{1,0:T(8,128)(2,1)S(1)}, bf16[32,4096]{1,0:T(8,128)(2,1)S(1)}, u32[]{:S(2)}, u32[]{:S(2)}) collective-permute-start(bf16[32,4096]{1,0:T(8,128)(2,1)S(1)} %get-tuple-element.7), channel_id=1, source_target_pairs={{0,8},{8,16},{16,24},{1,9},{9,17},{17,25},{2,10},{10,18},{18,26},{... | collective-permute-start | bytes 786440 | tf_op jit(solution)/shard_map/ppermute | solution.py:15
Sparse Core Ops, SparseCore 0:
  25.0 29.9 reduce-scatter.4
  65.5 27.8 all-gather.6
  103.8 26.6 reduce-scatter.6
  141.0 27.8 all-gather.8
  179.3 26.6 reduce-scatter.8
  208.9 8.2 all-gather.10
  219.0 72.1 all-gather.12
  302.1 43.6 reduce-scatter.10
